TPU v7x, 32 devices: a whole 2x2x4 slice. The times are simulated.
32 devices in a mesh: rows: 8 (over y, x, core), tp: 4 (over z).
Axes of the slice: x: 2, y: 2, z: 4, core: 2. Of those that a mesh axis runs over, the one named last changes fastest.
Arguments:
- features: bfloat16 [16384, 768], P('rows'), may hold values from -6 to 6
- type_ids: int32 [16384], P('rows'), may hold values 0 or 1
- segment_ids: int32 [32, 512], P('rows'), may hold values from 0 to 3, never falling along the last dimension, each value on 1 to 256 neighbouring positions
- type_table: bfloat16 [2, 768], replicated, may hold values from -3 to 3
- w_qkv: bfloat16 [3, 768, 768], P(None, None, 'tp'), may hold values from -0.3125 to 0.3125
- b_qv: bfloat16 [2, 768], P(None, 'tp'), may hold values from -3 to 3
- w_out: bfloat16 [768, 768], P('tp'), may hold values from -0.875 to 0.875
- b_out: bfloat16 [768], replicated, may hold values from -3 to 3
- gain_attn: bfloat16 [768], replicated, may hold values from 0.25 to 1.75
- shift_attn: bfloat16 [768], replicated, may hold values from -3 to 3
- w_up: bfloat16 [768, 3072], P(None, 'tp'), may hold values from -0.21875 to 0.21875
- b_up: bfloat16 [3072], P('tp'), may hold values from -3 to 3
- w_down: bfloat16 [3072, 768], P('tp'), may hold values from -0.109375 to 0.109375
- b_down: bfloat16 [768], replicated, may hold values from -3 to 3
- gain_ffn: bfloat16 [768], replicated, may hold values from 0.25 to 1.75
- shift_ffn: bfloat16 [768], replicated, may hold values from -3 to 3
- cotangent: bfloat16 [16384, 768], P('rows'), may hold values from -6 to 6
Outputs:
- output: bfloat16 [16384, 768], P('rows')
- grad_features: bfloat16 [16384, 768], P('rows')
- grad_table: float32 [2, 768], replicated
- grad_qkv: float32 [3, 768, 768], P(None, None, 'tp')
- grad_bias_qv: float32 [2, 768], P(None, 'tp')
- grad_w_out: float32 [768, 768], P('tp')
- grad_b_out: float32 [768], replicated
- grad_gain_attn: float32 [768], replicated
- grad_shift_attn: float32 [768], replicated
- grad_w_up: float32 [768, 3072], P(None, 'tp')
- grad_b_up: float32 [3072], P('tp')
- grad_w_down: float32 [3072, 768], P('tp')
- grad_b_down: float32 [768], replicated
- grad_gain_ffn: float32 [768], replicated
- grad_shift_ffn: float32 [768], replicated
Inputs may be any that keep to these rules, and one draw needn't show every extreme that they name: `segment_ids`: along each packed row the ids never fall; each of the 4 ids covers 1 to 256 tokens, and one covers exactly 256.
All inputs are finite; a program needn't handle non-finite values. No bound on the sum of `type_ids` on one device may be relied on, other than what follows from the above.
Results may differ from a plain program's by a relative error of at most 0.015.
The roundings to bfloat16 on the way count: a program that leaves them out, or rounds other values in their place, can miss the bound.
Values sent between devices are 32-bit elements; how exact they have to be, the bound alone decides.
No kernel may reach another device: no remote copies, remote signals or barrier semaphores. Data moves between devices by JAX's collectives and lax.ppermute only.
A program may use at most 128 MiB of HBM per device.

v0:
```python
from functools import partial
import jax
import jax.numpy as jnp
from jax import lax
from jax.sharding import PartitionSpec as P

HEAD_DIM = 64


def normalize(hidden):
    center = hidden - jnp.mean(hidden, axis=-1, keepdims=True)
    variance = jnp.mean(center * center, axis=-1, keepdims=True)
    inverse = lax.rsqrt(variance + 1e-05)
    return (center * inverse, inverse)


def norm_back(grad_norm, normed, inverse):
    mean_grad = jnp.mean(grad_norm, axis=-1, keepdims=True)
    mean_proj = jnp.mean(grad_norm * normed, axis=-1, keepdims=True)
    return inverse * (grad_norm - mean_grad - normed * mean_proj)


def counted_scores(queries, keys_row, segment):
    scale = queries.shape[-1] ** (-0.5)
    scores = (
        jnp.einsum("qhd,khd->hqk", queries, keys_row, preferred_element_type=jnp.float32) * scale
    )
    same_doc = segment[:, None] == segment[None, :]
    return (jnp.where(same_doc[None], scores, -1000000000.0), scale)


def attend_forward(packed):
    queries, keys_row, values, segment = packed
    masked, scale = counted_scores(queries, keys_row, segment)
    highest_score = jnp.max(masked, axis=-1, keepdims=True)
    weights = jnp.exp(masked - highest_score)
    total = jnp.sum(weights, axis=-1, keepdims=True)
    weights = weights / total
    attended = jnp.einsum(
        "hqk,khd->qhd", weights.astype(jnp.bfloat16), values, preferred_element_type=jnp.float32
    ).astype(jnp.bfloat16)
    return (attended, highest_score[..., 0] + jnp.log(total[..., 0]))


def attend_backward(packed):
    queries, keys_row, values, segment, logsum, grad_attended = packed
    masked, scale = counted_scores(queries, keys_row, segment)
    weights = jnp.exp(masked - logsum[..., None])
    grad_weights = jnp.einsum(
        "qhd,khd->hqk", grad_attended, values, preferred_element_type=jnp.float32
    )
    inner = jnp.sum(weights * grad_weights, axis=-1, keepdims=True)
    grad_scores = (weights * (grad_weights - inner)).astype(jnp.bfloat16)
    grad_queries = (
        jnp.einsum("hqk,khd->qhd", grad_scores, keys_row, preferred_element_type=jnp.float32)
        * scale
    )
    grad_keys = (
        jnp.einsum("hqk,qhd->khd", grad_scores, queries, preferred_element_type=jnp.float32) * scale
    )
    grad_values = jnp.einsum(
        "hqk,qhd->khd",
        weights.astype(jnp.bfloat16),
        grad_attended,
        preferred_element_type=jnp.float32,
    )
    return (grad_queries, grad_keys, grad_values)


def per_device(
    features,
    type_ids,
    segment_ids,
    type_table,
    w_qkv,
    b_qv,
    w_out,
    b_out,
    gain_attn,
    shift_attn,
    w_up,
    b_up,
    w_down,
    b_down,
    gain_ffn,
    shift_ffn,
    cotangent,
):
    tokens = features.shape[0]
    packed_rows = segment_ids.shape[0]
    length = segment_ids.shape[1]
    local_width = w_qkv.shape[2]
    local_heads = local_width // HEAD_DIM
    shape_four = (packed_rows, length, local_heads, HEAD_DIM)
    type_frac = type_ids.astype(jnp.float32)[:, None]
    table = type_table.astype(jnp.float32)
    embedded = features.astype(jnp.float32) + (table[0] + type_frac * (table[1] - table[0]))
    normal_in = embedded.astype(jnp.bfloat16)
    projected = jnp.einsum("nd,sdc->snc", normal_in, w_qkv, preferred_element_type=jnp.float32)
    bias_qv = b_qv.astype(jnp.float32)
    queries = (projected[0] + bias_qv[0]).astype(jnp.bfloat16).reshape(shape_four)
    keys_all = projected[1].astype(jnp.bfloat16).reshape(shape_four)
    values = (projected[2] + bias_qv[1]).astype(jnp.bfloat16).reshape(shape_four)
    attended, logsum = lax.map(attend_forward, (queries, keys_all, values, segment_ids))
    attended = attended.reshape(tokens, local_width)
    attn_part = jnp.dot(attended, w_out, preferred_element_type=jnp.float32)
    attn_out = lax.psum(attn_part, "tp") + b_out.astype(jnp.float32)
    h_one = embedded + attn_out
    normed_a, inverse_a = normalize(h_one)
    gain_one = gain_attn.astype(jnp.float32)
    normed_one = normed_a * gain_one + shift_attn.astype(jnp.float32)
    ffn_in = normed_one.astype(jnp.bfloat16)
    pre_act = jnp.dot(ffn_in, w_up, preferred_element_type=jnp.float32) + b_up.astype(jnp.float32)
    activated = jax.nn.gelu(pre_act, approximate=False).astype(jnp.bfloat16)
    ffn_part = jnp.dot(activated, w_down, preferred_element_type=jnp.float32)
    ffn_out = lax.psum(ffn_part, "tp") + b_down.astype(jnp.float32)
    h_two = normed_one + ffn_out
    normed_b, inverse_b = normalize(h_two)
    gain_two = gain_ffn.astype(jnp.float32)
    output = (normed_b * gain_two + shift_ffn.astype(jnp.float32)).astype(jnp.bfloat16)
    grad_out = cotangent.astype(jnp.float32)
    grad_shift_ffn = jnp.sum(grad_out, axis=0)
    grad_gain_ffn = jnp.sum(grad_out * normed_b, axis=0)
    grad_h2 = norm_back(grad_out * gain_two, normed_b, inverse_b)
    grad_b_down = jnp.sum(grad_h2, axis=0)
    grad_h2_low = grad_h2.astype(jnp.bfloat16)
    grad_w_down = jnp.einsum(
        "nf,nd->fd", activated, grad_h2_low, preferred_element_type=jnp.float32
    )
    grad_act = jnp.einsum("nd,fd->nf", grad_h2_low, w_down, preferred_element_type=jnp.float32)
    unused_value, gelu_pull = jax.vjp(partial(jax.nn.gelu, approximate=False), pre_act)
    grad_pre = gelu_pull(grad_act)[0].astype(jnp.bfloat16)
    grad_b_up = jnp.sum(grad_pre.astype(jnp.float32), axis=0)
    grad_w_up = jnp.einsum("nd,nf->df", ffn_in, grad_pre, preferred_element_type=jnp.float32)
    ffn_grads = (grad_w_up, grad_b_up, grad_w_down, grad_b_down, grad_gain_ffn, grad_shift_ffn)
    grad_in_part = jnp.einsum("nf,df->nd", grad_pre, w_up, preferred_element_type=jnp.float32)
    grad_normed = grad_h2 + lax.psum(grad_in_part, "tp")
    grad_shift_attn = jnp.sum(grad_normed, axis=0)
    grad_gain_attn = jnp.sum(grad_normed * normed_a, axis=0)
    grad_h1 = norm_back(grad_normed * gain_one, normed_a, inverse_a)
    grad_b_out = jnp.sum(grad_h1, axis=0)
    grad_h1_low = grad_h1.astype(jnp.bfloat16)
    grad_w_out = jnp.einsum("nc,nd->cd", attended, grad_h1_low, preferred_element_type=jnp.float32)
    grad_attended = jnp.einsum("nd,cd->nc", grad_h1_low, w_out, preferred_element_type=jnp.float32)
    grad_attended = grad_attended.astype(jnp.bfloat16).reshape(shape_four)
    grad_queries, grad_keys, grad_values = lax.map(
        attend_backward, (queries, keys_all, values, segment_ids, logsum, grad_attended)
    )
    grad_proj = jnp.stack(
        [
            grad_queries.reshape(tokens, local_width),
            grad_keys.reshape(tokens, local_width),
            grad_values.reshape(tokens, local_width),
        ]
    ).astype(jnp.bfloat16)
    grad_bias_qv = jnp.sum(grad_proj[0::2].astype(jnp.float32), axis=1)
    grad_qkv = jnp.einsum("nd,snc->sdc", normal_in, grad_proj, preferred_element_type=jnp.float32)
    grad_embed_part = jnp.einsum(
        "snc,sdc->nd", grad_proj, w_qkv, preferred_element_type=jnp.float32
    )
    grad_embedded = grad_h1 + lax.psum(grad_embed_part, "tp")
    grad_features = grad_embedded.astype(jnp.bfloat16)
    grad_upper = jnp.sum(type_frac * grad_embedded, axis=0)
    grad_lower = jnp.sum(grad_embedded, axis=0) - grad_upper
    grad_table = jnp.stack([grad_lower, grad_upper])
    attn_grads = (
        grad_table,
        grad_qkv,
        grad_bias_qv,
        grad_w_out,
        grad_b_out,
        grad_gain_attn,
        grad_shift_attn,
    )
    summed = lax.psum(
        (
            grad_table,
            grad_qkv,
            grad_bias_qv,
            grad_w_out,
            grad_b_out,
            grad_gain_attn,
            grad_shift_attn,
            grad_w_up,
            grad_b_up,
            grad_w_down,
            grad_b_down,
            grad_gain_ffn,
            grad_shift_ffn,
        ),
        "rows",
    )
    attn_grads = summed[:7]
    ffn_grads = summed[7:]
    return (
        output,
        grad_features,
        attn_grads[0],
        attn_grads[1],
        attn_grads[2],
        attn_grads[3],
        attn_grads[4],
        attn_grads[5],
        attn_grads[6],
        ffn_grads[0],
        ffn_grads[1],
        ffn_grads[2],
        ffn_grads[3],
        ffn_grads[4],
        ffn_grads[5],
    )


def solution(mesh):
    in_specs = (
        P("rows", None),
        P("rows"),
        P("rows", None),
        P(),
        P(None, None, "tp"),
        P(None, "tp"),
        P("tp", None),
        P(),
        P(),
        P(),
        P(None, "tp"),
        P("tp"),
        P("tp", None),
        P(),
        P(),
        P(),
        P("rows", None),
    )
    out_specs = (
        P("rows", None),
        P("rows", None),
        P(),
        P(None, None, "tp"),
        P(None, "tp"),
        P("tp", None),
        P(),
        P(),
        P(),
        P(None, "tp"),
        P("tp"),
        P("tp", None),
        P(),
        P(),
        P(),
    )
    return jax.shard_map(
        per_device, mesh=mesh, in_specs=in_specs, out_specs=out_specs, check_vma=False
    )
```

profile of v0, /device:TPU:0, one launch (start us, length us, event | category | flops | bytes accessed | tf_op | source)
XLA Modules:
  0.0 1206.2 jit_solution(2927941638229971674)
XLA Ops:
  8.8 4.3 fusion.81
  13.0 1.4 fusion.89
  14.5 3.1 squeeze.36
  17.7 2.2 squeeze.37
  22.6 2.9 fusion.66
  25.6 19.1 %while.26 = (s32[]{:T(128)}, bf16[4,512,3,64]{1,3,2,0:T(8,128)(2,1)}, f32[4,3,512]{2,1,0:T(4,128)}, bf16[4,512,3,64]{1,3,2,0:T(8,128)(2,1)S(1)}, s32[4,512]{1,0:...) while((s32[]{:T(128)}, ...), condition=%wide.region_3.4_spmd, body=%wide.region_0.3_spmd.sunk | while | flops 211122688 | bytes 11336281 | solution.py:104
  28.6 1.8 fusion.133
  33.4 1.8 fusion.133
  38.1 1.8 fusion.133
  42.9 1.8 fusion.133
  44.7 1.7 copy.51
  47.5 4.7 fusion.90
  57.5 220.4 %all-reduce.8.cloned.1.call-done = f32[2048,768]{1,0:T(8,128)} async-done(((f32[2048,768]{1,0:T(8,128)}), f32[2048,768]{1,0:T(8,128)}) %all-reduce.8.cloned.1.call-update) | async-done | bytes 6291472 | tf_op jit(solution)/shard_map/psum | solution.py:107
  277.9 4.8 fusion.88
  285.4 18.4 %multiply_convert_fusion.1 = (bf16[2048,768]{1,0:T(8,128)(2,1)S(1)}, f32[2048,768]{1,0:T(8,128)}, f32[2048,768]{1,0:T(8,128)}) fusion(f32[768]{0:T(1024)S(1)} %copy-done.38, bf16[2048,768]{1,0:T(8,128)(2,1)S(1)} %fusion.63, bf16[768,768]{1,0:T(8,128)(2,1)S(1)} %copy-done), kind=kOutput, calls=%fused_computation.80 | convolution fusion | flops 2519728128 | bytes 20057088 | tf_op jit(solution)/shard_map/dot_general | solution.py:113
  303.8 1.6 copy-done.10
  305.5 4.6 fusion.91
  313.9 218.0 %all-reduce.10.cloned.1.call-done = f32[2048,768]{1,0:T(8,128)} async-done(((f32[2048,768]{1,0:T(8,128)}), f32[2048,768]{1,0:T(8,128)}) %all-reduce.10.cloned.1.call-update) | async-done | bytes 6291472 | tf_op jit(solution)/shard_map/psum | solution.py:116
  531.9 5.7 fusion.86
  539.5 3.6 fusion.56
  543.2 4.5 fusion.84
  547.7 9.5 convert_reduce_fusion.1
  557.2 1.8 copy-done.42
  559.0 4.5 fusion.92
  563.8 221.6 %all-reduce.12.cloned.1.call-done = f32[2048,768]{1,0:T(8,128)} async-done(((f32[2048,768]{1,0:T(8,128)}), f32[2048,768]{1,0:T(8,128)}) %all-reduce.12.cloned.1.call-update) | async-done | bytes 6291472 | tf_op jit(solution)/shard_map/psum | solution.py:137
  785.4 8.7 multiply_reduce_fusion.1
  794.2 4.5 subtract_multiply_fusion
  798.7 2.6 copy-done.3
  802.6 1.5 reshape.196
  804.0 1.3 copy.53
  805.3 30.2 %while.27 = (s32[]{:T(128)}, bf16[4,512,3,64]{1,3,2,0:T(8,128)(2,1)}, bf16[4,512,3,64]{1,3,2,0:T(8,128)(2,1)}, bf16[4,512,3,64]{1,3,2,0:T(8,128)(2,1)}, bf16[4,5...) while((s32[]{:T(128)}, ...), condition=%wide.region_17.18_spmd, body=%wide.region_15.17_spmd.sunk | while | flops 510851584 | bytes 39300324 | solution.py:146
  835.5 1.7 copy.54
  838.8 1.7 copy.55
  841.2 1.7 copy.56
  845.4 7.1 convolution_bitcast_fusion
  852.8 7.1 fusion.93
  859.9 7.0 fusion.71
  866.9 4.5 fusion.68
  871.5 3.5 fusion.77
  875.0 1.6 copy-done.13
  877.0 197.4 %all-reduce.14.cloned.1.call-done = f32[2048,768]{1,0:T(8,128)} async-done(((f32[2048,768]{1,0:T(8,128)}), f32[2048,768]{1,0:T(8,128)}) %all-reduce.14.cloned.1.call-update) | async-done | bytes 6291472 | tf_op jit(solution)/shard_map/psum | solution.py:161
  1074.5 6.9 add_reduce_fusion
  1081.5 27.2 %all-reduce = (f32[2,768]{1,0:T(2,128)}, f32[2,192]{1,0:T(2,128)}, f32[768]{0:T(1024)}, f32[768]{0:T(1024)}, f32[768]{0:T(1024)}, /*index=5*/f32[768]{0:T(1024)}, f32[768]{0:T(1024)}, f32[768]{0:T(1024)}, f32[768]{0:T(1024)}) all-reduce(f32[2,768]{1,0:T(2,128)S(1)} %pad_maximum_fusion, ...), channel_id=1, replica_groups=mesh['rows'=8,'tp'=4] {'rows'}, use_global_device_ids=true, to_apply=%region_21.22 | all-reduce | flops 7296 | bytes 58368 | tf_op jit(solution)/shard_map/psum | solution.py:175
  1108.7 83.1 %all-reduce.16.cloned.1.call-done = (f32[3,768,192]{1,2,0:T(8,128)}, f32[192,768]{1,0:T(8,128)}, f32[768,768]{1,0:T(8,128)}, f32[768,768]{1,0:T(8,128)}) async-done(((f32[3,768,192]{1,2,0:T(8,128)}, f32[192,768]{1,0:T(8,128)}, f32[768,768]{1,0:T(8,128)}, f32[768,768]{1,0:T(8,128)}), (f32[3,768,192]{1,2,0:T(8,128)}, f32[192,768]{1,0:T(8,128)}, f32[768,768]{1,0:T(8,128)}, ...) | async-done | bytes 7077904 | tf_op jit(solution)/shard_map/psum | solution.py:175
  1191.8 2.9 copy.106
  1194.7 1.9 copy.107
  1196.7 1.4 copy.108
  1198.1 1.4 copy.109
  (222 shorter events, 67.4 us)
Async XLA Ops:
  7.2 278.2 %copy-start = (bf16[768,768]{1,0:T(8,128)(2,1)S(1)}, bf16[768,768]{1,0:T(8,128)(2,1)}, u32[]{:S(2)}) copy-start(bf16[768,768]{1,0:T(8,128)(2,1)} %param.31) | copy-start | bytes 3538948
  7.2 270.7 %all-reduce.8.cloned.1.call-start = ((), (), s32[]{:S(2)}) async-start(), calls=%async_computation | async-start | bytes 12582912 | tf_op jit(solution)/shard_map/psum | solution.py:107
  8.0 269.9 %copy-start.29 = (f32[768]{0:T(1024)}, f32[768]{0:T(1024)S(1)}, u32[]{:S(2)}) copy-start(f32[768]{0:T(1024)S(1)} %get-tuple-element.157) | copy-start | bytes 9220
  8.1 269.9 %copy-start.31 = (f32[768]{0:T(1024)}, f32[768]{0:T(1024)S(1)}, u32[]{:S(2)}) copy-start(f32[768]{0:T(1024)S(1)} %get-tuple-element.158) | copy-start | bytes 9220
  8.8 269.2 %copy-start.23 = (f32[2048]{0:T(1024)}, f32[2048]{0:T(1024)S(1)}, u32[]{:S(2)}) copy-start(f32[2048]{0:T(1024)S(1)} %convert_element_type.100) | copy-start | bytes 24580
  52.2 479.7 %all-reduce.10.cloned.1.call-start = ((), (), s32[]{:S(2)}) async-start(), calls=%async_computation.1 | async-start | bytes 12582912 | tf_op jit(solution)/shard_map/psum | solution.py:116
  282.7 2.7 copy-start.2
  283.6 1.8 copy-start.38
  285.4 18.5 %copy-start.9 = (bf16[2048,768]{1,0:T(8,128)(2,1)}, bf16[2048,768]{1,0:T(8,128)(2,1)S(1)}, u32[]{:S(2)}) copy-start(bf16[2048,768]{1,0:T(8,128)(2,1)S(1)} %fusion.63) | copy-start | bytes 9437188
  285.4 20.1 %copy-start.40 = (bf16[768,768]{1,0:T(8,128)(2,1)S(1)}, bf16[768,768]{1,0:T(8,128)(2,1)}, u32[]{:S(2)}) copy-start(bf16[768,768]{1,0:T(8,128)(2,1)} %param.33) | copy-start | bytes 3538948
  303.8 1.6 copy-start.10
  310.0 475.4 %all-reduce.12.cloned.1.call-start = ((), (), s32[]{:S(2)}) async-start(), calls=%async_computation.2 | async-start | bytes 12582912 | tf_op jit(solution)/shard_map/psum | solution.py:137
  537.6 1.9 copy-start.5
  537.7 1.9 copy-start.25
  538.5 4.6 copy-start.36
  539.5 8.1 slice-start
  543.2 4.5 copy-start.39
  543.2 4.5 copy-start.41
  543.2 4.5 slice-start.1
  547.7 9.5 copy-start.4
  557.2 1.8 copy-start.42
  563.5 221.9 %copy-start.22 = (f32[768]{0:T(1024)S(1)}, f32[768]{0:T(1024)}, u32[]{:S(2)}) copy-start(f32[768]{0:T(1024)} %convert_element_type.107) | copy-start | bytes 9220
  563.5 510.9 %all-reduce.14.cloned.1.call-start = ((), (), s32[]{:S(2)}) async-start(), calls=%async_computation.3 | async-start | bytes 12582912 | tf_op jit(solution)/shard_map/psum | solution.py:161
  794.2 7.2 copy-start.16
  798.7 2.7 copy-start.3
  807.6 2.0 copy-start.19
  808.7 1.5 copy-start.17
  815.0 2.0 copy-start.19
  822.5 2.0 copy-start.19
  829.9 2.0 copy-start.19
  852.6 339.2 %all-reduce.16.cloned.1.call-start = ((), (), s32[]{:S(2)}) async-start(), calls=%async_computation.4 | async-start | bytes 14155776 | tf_op jit(solution)/shard_map/psum | solution.py:175
  852.8 7.1 copy-start.11
  859.9 7.1 copy-start.7
  866.9 4.6 copy-start.8
  866.9 4.6 copy-start.12
  866.9 4.6 copy-start.24
  866.9 4.6 copy-start.30
  866.9 4.6 copy-start.32
  875.0 1.7 copy-start.13
  877.0 204.4 %copy-start.27 = (f32[768]{0:T(1024)S(1)}, f32[768]{0:T(1024)}, u32[]{:S(2)}) copy-start(f32[768]{0:T(1024)} %get-tuple-element.150) | copy-start | bytes 9220
  877.0 204.4 %copy-start.28 = (f32[768]{0:T(1024)S(1)}, f32[768]{0:T(1024)}, u32[]{:S(2)}) copy-start(f32[768]{0:T(1024)} %get-tuple-element.156) | copy-start | bytes 9220
  877.0 204.4 %copy-start.33 = (f32[768]{0:T(1024)S(1)}, f32[768]{0:T(1024)}, u32[]{:S(2)}) copy-start(f32[768]{0:T(1024)} %get-tuple-element.208) | copy-start | bytes 9220
  877.0 204.4 %copy-start.34 = (f32[768]{0:T(1024)S(1)}, f32[768]{0:T(1024)}, u32[]{:S(2)}) copy-start(f32[768]{0:T(1024)} %get-tuple-element.146) | copy-start | bytes 9220
  877.0 204.4 %copy-start.35 = (f32[768]{0:T(1024)S(1)}, f32[768]{0:T(1024)}, u32[]{:S(2)}) copy-start(f32[768]{0:T(1024)} %get-tuple-element.153) | copy-start | bytes 9220
  877.0 204.4 %copy-start.37 = (f32[768]{0:T(1024)S(1)}, f32[768]{0:T(1024)}, u32[]{:S(2)}) copy-start(f32[768]{0:T(1024)} %get-tuple-element.226) | copy-start | bytes 9220
  1191.8 4.9 copy-start.15
  1191.8 6.3 copy-start.14
  1191.8 7.7 copy-start.1
  (14 other events, 15.9 us)
Sparse Core Ops, SparseCore 0:
  52.3 225.5 all-reduce.7
  310.2 221.7 all-reduce.9
  563.6 221.7 all-reduce.11
  852.7 221.7 all-reduce.13
  1079.1 112.6 all-reduce.15
where the time goes:
time: 1220 us; the launch traced here: 1210 us
  waiting for transfers between devices  941 us (77%)
  matrix products  103 us (8%)
  other arithmetic  66.3 us (5%)
  local copies, waits for them, and re-layouts  53.4 us (4%)
  blocking collectives  27.2 us (2%)
  between operations  14.5 us (1%)
    psum x1, waiting for transfers between devices, per_device(): grad_normed = grad_h2 + lax.psum(grad_in_part, 'tp')  222 us
    psum x1, waiting for transfers between devices, per_device(): attn_out = lax.psum(attn_part, 'tp') + b_out.astype(jnp.float32)  220 us
    psum x1, waiting for transfers between devices, per_device(): ffn_out = lax.psum(ffn_part, 'tp') + b_down.astype(jnp.float32)  218 us
    psum x1, waiting for transfers between devices, per_device(): grad_embedded = grad_h1 + lax.psum(grad_embed_part, 'tp')  197 us
    psum x1, waiting for transfers between devices, per_device(): lax.psum((grad_table, grad_qkv, grad_bias_qv, grad_w_out, grad_b_out, gra...  83.1 us
    psum x1, blocking collectives, per_device(): lax.psum((grad_table, grad_qkv, grad_bias_qv, grad_w_out, grad_b_out, gra...  27.2 us
  transfers between devices with their start and end apart: 5, of which 5 were waited for; matrix products, arithmetic and copies ran while one was open for 3% of the time, Pallas kernels for 0%

commit v1 on v0

--- a/solution.py
+++ b/solution.py
@@ -104,7 +104,7 @@
     attended, logsum = lax.map(attend_forward, (queries, keys_all, values, segment_ids))
     attended = attended.reshape(tokens, local_width)
     attn_part = jnp.dot(attended, w_out, preferred_element_type=jnp.float32)
-    attn_out = lax.psum(attn_part, "tp") + b_out.astype(jnp.float32)
+    attn_out = jnp.sum(lax.all_gather(attn_part, "tp"), axis=0) + b_out.astype(jnp.float32)
     h_one = embedded + attn_out
     normed_a, inverse_a = normalize(h_one)
     gain_one = gain_attn.astype(jnp.float32)

time: 1220 us -> 1430 us (1.17)
  waiting for transfers between devices: 941 us -> 1150 us
    all_gather x0 -> x1, waiting for transfers between devices: none -> 427 us  [per_device(): lax.all_gather(attn_part, 'tp')]
    psum x1 -> x0, waiting for transfers between devices: 220 us -> none  [per_device(): attn_out = lax.psum(attn_part, 'tp') + b_out.astype(jnp.float32)]
  transfers between devices with their start and end apart: 5 -> 5, of which waited for: 5 -> 5; matrix products, arithmetic and copies ran while one was open for 3% -> 2% of each run, Pallas kernels for 0% -> 0%
where the time goes in v1:
time: 1430 us; the launch traced here: 1420 us
  waiting for transfers between devices  1150 us (80%)
  matrix products  106 us (7%)
  other arithmetic  70 us (5%)
  local copies, waits for them, and re-layouts  47 us (3%)
  blocking collectives  27.2 us (2%)
  between operations  14.8 us (1%)
    all_gather x1, waiting for transfers between devices, per_device(): lax.all_gather(attn_part, 'tp')  427 us
    psum x1, waiting for transfers between devices, per_device(): grad_normed = grad_h2 + lax.psum(grad_in_part, 'tp')  222 us
    psum x1, waiting for transfers between devices, per_device(): ffn_out = lax.psum(ffn_part, 'tp') + b_down.astype(jnp.float32)  220 us
    psum x1, waiting for transfers between devices, per_device(): grad_embedded = grad_h1 + lax.psum(grad_embed_part, 'tp')  199 us
    psum x1, waiting for transfers between devices, per_device(): lax.psum((grad_table, grad_qkv, grad_bias_qv, grad_w_out, grad_b_out, gra...  83.1 us
  transfers between devices with their start and end apart: 5, of which 5 were waited for; matrix products, arithmetic and copies ran while one was open for 2% of the time, Pallas kernels for 0%

profile of v1, /device:TPU:0, one launch (start us, length us, event | category | flops | bytes accessed | tf_op | source)
XLA Modules:
  0.0 1419.1 jit_solution(12289100574777248695)
XLA Ops:
  8.8 4.3 fusion.81
  14.6 3.1 squeeze.36
  17.8 2.2 squeeze.37
  22.7 2.9 fusion.66
  25.7 16.3 %while.26 = (s32[]{:T(128)}, bf16[4,512,3,64]{1,3,2,0:T(8,128)(2,1)}, f32[4,3,512]{2,1,0:T(4,128)}, bf16[4,512,3,64]{1,3,2,0:T(8,128)(2,1)S(1)}, s32[4,512]{1,0:...) while((s32[]{:T(128)}, ...), condition=%wide.region_3.4_spmd, body=%wide.region_0.3_spmd.sunk | while | flops 211122688 | bytes 11336281 | solution.py:104
  28.0 1.8 fusion.133
  32.1 1.8 fusion.133
  36.2 1.8 fusion.133
  40.3 1.8 fusion.133
  42.0 2.0 copy.51
  45.1 4.7 fusion.90
  50.6 427.3 %all-gather.3.cloned.1.call-done = f32[8192,768]{1,0:T(8,128)} async-done(((f32[2048,768]{1,0:T(8,128)}), f32[8192,768]{1,0:T(8,128)}) %all-gather.3.cloned.1.call-update) | async-done | bytes 25165840 | tf_op jit(solution)/shard_map/all_gather | solution.py:107
  477.9 12.7 reduce_sum.193
  490.6 4.7 fusion.88
  498.0 18.4 %multiply_convert_fusion.1 = (bf16[2048,768]{1,0:T(8,128)(2,1)S(1)}, f32[2048,768]{1,0:T(8,128)}, f32[2048,768]{1,0:T(8,128)}) fusion(f32[768]{0:T(1024)S(1)} %convert_element_type.110, bf16[2048,768]{1,0:T(8,128)(2,1)S(1)} %fusion.63, bf16[768,768]{1,0:T(8,128)(2,1)S(1)} %copy-done), kind=kOutput, calls=%fused_computation.80 | convolution fusion | flops 2519728128 | bytes 20057088 | tf_op jit(solution)/shard_map/dot_general | solution.py:113
  516.5 1.6 copy-done.10
  518.1 4.6 fusion.91
  523.4 220.5 %all-reduce.7.cloned.1.call-done = f32[2048,768]{1,0:T(8,128)} async-done(((f32[2048,768]{1,0:T(8,128)}), f32[2048,768]{1,0:T(8,128)}) %all-reduce.7.cloned.1.call-update) | async-done | bytes 6291472 | tf_op jit(solution)/shard_map/psum | solution.py:116
  743.9 5.7 fusion.86
  751.5 3.6 fusion.56
  755.1 4.5 fusion.84
  759.6 9.5 convert_reduce_fusion.1
  769.1 1.8 copy-done.44
  770.9 4.5 fusion.92
  775.7 221.6 %all-reduce.9.cloned.1.call-done = f32[2048,768]{1,0:T(8,128)} async-done(((f32[2048,768]{1,0:T(8,128)}), f32[2048,768]{1,0:T(8,128)}) %all-reduce.9.cloned.1.call-update) | async-done | bytes 6291472 | tf_op jit(solution)/shard_map/psum | solution.py:137
  997.3 8.7 multiply_reduce_fusion.1
  1006.1 4.5 subtract_multiply_fusion
  1010.6 2.6 copy-done.2
  1014.5 1.5 reshape.196
  1017.2 31.0 %while.27 = (s32[]{:T(128)}, bf16[4,512,3,64]{1,3,2,0:T(8,128)(2,1)}, bf16[4,512,3,64]{1,3,2,0:T(8,128)(2,1)}, bf16[4,512,3,64]{1,3,2,0:T(8,128)(2,1)}, bf16[4,5...) while((s32[]{:T(128)}, ...), condition=%wide.region_17.18_spmd, body=%wide.region_15.17_spmd.sunk | while | flops 510851584 | bytes 39300324 | solution.py:146
  1017.3 1.5 fusion.142
  1024.9 1.5 fusion.142
  1032.6 1.5 fusion.142
  1040.3 1.5 fusion.142
  1048.2 1.7 copy.54
  1051.5 1.7 copy.55
  1053.8 1.7 copy.56
  1058.0 7.1 convolution_bitcast_fusion
  1065.5 7.1 fusion.93
  1072.6 7.0 fusion.71
  1079.7 4.6 fusion.68
  1084.3 3.5 fusion.77
  1088.2 198.9 %all-reduce.11.cloned.1.call-done = f32[2048,768]{1,0:T(8,128)} async-done(((f32[2048,768]{1,0:T(8,128)}), f32[2048,768]{1,0:T(8,128)}) %all-reduce.11.cloned.1.call-update) | async-done | bytes 6291472 | tf_op jit(solution)/shard_map/psum | solution.py:161
  1287.1 6.9 add_reduce_fusion
  1294.1 27.2 %all-reduce = (f32[2,768]{1,0:T(2,128)}, f32[2,192]{1,0:T(2,128)}, f32[768]{0:T(1024)}, f32[768]{0:T(1024)}, f32[768]{0:T(1024)}, /*index=5*/f32[768]{0:T(1024)}, f32[768]{0:T(1024)}, f32[768]{0:T(1024)}, f32[768]{0:T(1024)}) all-reduce(f32[2,768]{1,0:T(2,128)S(1)} %pad_maximum_fusion, ...), channel_id=1, replica_groups=mesh['rows'=8,'tp'=4] {'rows'}, use_global_device_ids=true, to_apply=%region_21.22 | all-reduce | flops 7296 | bytes 58368 | tf_op jit(solution)/shard_map/psum | solution.py:175
  1321.3 83.1 %all-reduce.13.cloned.1.call-done = (f32[3,768,192]{1,2,0:T(8,128)}, f32[192,768]{1,0:T(8,128)}, f32[768,768]{1,0:T(8,128)}, f32[768,768]{1,0:T(8,128)}) async-done(((f32[3,768,192]{1,2,0:T(8,128)}, f32[192,768]{1,0:T(8,128)}, f32[768,768]{1,0:T(8,128)}, f32[768,768]{1,0:T(8,128)}), (f32[3,768,192]{1,2,0:T(8,128)}, f32[192,768]{1,0:T(8,128)}, f32[768,768]{1,0:T(8,128)}, ...) | async-done | bytes 7077904 | tf_op jit(solution)/shard_map/psum | solution.py:175
  1404.4 2.9 copy.105
  1407.4 1.9 copy.106
  (227 shorter events, 57.2 us)
Async XLA Ops:
  7.2 490.9 %copy-start = (bf16[768,768]{1,0:T(8,128)(2,1)S(1)}, bf16[768,768]{1,0:T(8,128)(2,1)}, u32[]{:S(2)}) copy-start(bf16[768,768]{1,0:T(8,128)(2,1)} %param.31) | copy-start | bytes 3538948
  7.2 470.7 %all-gather.3.cloned.1.call-start = ((), (), s32[]{:S(2)}) async-start(), calls=%async_computation.3 | async-start | bytes 31457280 | tf_op jit(solution)/shard_map/all_gather | solution.py:107
  8.0 5.0 copy-start.25
  8.1 5.0 copy-start.28
  8.8 481.9 %copy-start.20 = (f32[2048]{0:T(1024)}, f32[2048]{0:T(1024)S(1)}, u32[]{:S(2)}) copy-start(f32[2048]{0:T(1024)S(1)} %convert_element_type.100) | copy-start | bytes 24580
  17.7 7.9 copy-start.22
  42.0 7.8 copy-start.7
  49.9 694.0 %all-reduce.7.cloned.1.call-start = ((), (), s32[]{:S(2)}) async-start(), calls=%async_computation | async-start | bytes 12582912 | tf_op jit(solution)/shard_map/psum | solution.py:116
  477.9 12.7 copy-start.26
  477.9 12.7 copy-start.29
  495.4 2.7 copy-start.1
  498.0 18.4 %copy-start.9 = (bf16[2048,768]{1,0:T(8,128)(2,1)}, bf16[2048,768]{1,0:T(8,128)(2,1)S(1)}, u32[]{:S(2)}) copy-start(bf16[2048,768]{1,0:T(8,128)(2,1)S(1)} %fusion.63) | copy-start | bytes 9437188
  498.0 20.1 %copy-start.42 = (bf16[768,768]{1,0:T(8,128)(2,1)S(1)}, bf16[768,768]{1,0:T(8,128)(2,1)}, u32[]{:S(2)}) copy-start(bf16[768,768]{1,0:T(8,128)(2,1)} %param.33) | copy-start | bytes 3538948
  516.5 1.6 copy-start.10
  522.7 474.6 %all-reduce.9.cloned.1.call-start = ((), (), s32[]{:S(2)}) async-start(), calls=%async_computation.1 | async-start | bytes 12582912 | tf_op jit(solution)/shard_map/psum | solution.py:137
  749.6 1.9 copy-start.4
  751.5 8.1 slice-start
  755.1 4.5 copy-start.43
  755.1 4.5 slice-start.1
  759.6 9.5 copy-start.3
  769.1 1.8 copy-start.44
  775.4 511.6 %all-reduce.11.cloned.1.call-start = ((), (), s32[]{:S(2)}) async-start(), calls=%async_computation.2 | async-start | bytes 12582912 | tf_op jit(solution)/shard_map/psum | solution.py:161
  1006.1 7.2 copy-start.15
  1010.6 2.7 copy-start.2
  1019.7 2.0 copy-start.18
  1020.9 1.5 copy-start.16
  1027.4 2.0 copy-start.18
  1028.6 1.5 copy-start.16
  1035.1 2.0 copy-start.18
  1036.3 1.5 copy-start.16
  1042.8 2.0 copy-start.18
  1044.0 1.5 copy-start.16
  1065.2 339.2 %all-reduce.13.cloned.1.call-start = ((), (), s32[]{:S(2)}) async-start(), calls=%async_computation.4 | async-start | bytes 14155776 | tf_op jit(solution)/shard_map/psum | solution.py:175
  1065.5 7.1 copy-start.11
  1072.6 7.1 copy-start.6
  1079.7 4.6 copy-start.8
  1079.7 4.6 copy-start.12
  1079.7 4.6 copy-start.21
  1079.7 4.6 copy-start.27
  1079.7 4.6 copy-start.30
  1088.1 205.9 %copy-start.23 = (f32[768]{0:T(1024)S(1)}, f32[768]{0:T(1024)}, u32[]{:S(2)}) copy-start(f32[768]{0:T(1024)} %get-tuple-element.150) | copy-start | bytes 9220
  1088.1 205.9 %copy-start.24 = (f32[768]{0:T(1024)S(1)}, f32[768]{0:T(1024)}, u32[]{:S(2)}) copy-start(f32[768]{0:T(1024)} %get-tuple-element.156) | copy-start | bytes 9220
  1088.1 205.9 %copy-start.31 = (f32[768]{0:T(1024)S(1)}, f32[768]{0:T(1024)}, u32[]{:S(2)}) copy-start(f32[768]{0:T(1024)} %get-tuple-element.208) | copy-start | bytes 9220
  1088.1 205.9 %copy-start.32 = (f32[768]{0:T(1024)S(1)}, f32[768]{0:T(1024)}, u32[]{:S(2)}) copy-start(f32[768]{0:T(1024)} %get-tuple-element.146) | copy-start | bytes 9220
  1088.1 205.9 %copy-start.33 = (f32[768]{0:T(1024)S(1)}, f32[768]{0:T(1024)}, u32[]{:S(2)}) copy-start(f32[768]{0:T(1024)} %get-tuple-element.153) | copy-start | bytes 9220
  1088.1 205.9 %copy-start.34 = (f32[768]{0:T(1024)S(1)}, f32[768]{0:T(1024)}, u32[]{:S(2)}) copy-start(f32[768]{0:T(1024)} %get-tuple-element.226) | copy-start | bytes 9220
  1404.4 4.9 copy-start.14
  1404.4 6.3 copy-start.13
  (16 other events, 14.5 us)
Sparse Core Ops, SparseCore 0:
  50.0 427.8 all-gather.2
  522.8 221.0 all-reduce.6
  775.6 221.7 all-reduce.8
  1065.3 221.7 all-reduce.10
  1291.8 112.6 all-reduce.12
